TPU v7x, 256 devices: a whole 4x4x8 slice. The times are simulated.
256 devices in a mesh: dp: 8 (over y, core), seq: 32 (over z, x).
Axes of the slice: x: 4, y: 4, z: 8, core: 2. Of those that a mesh axis runs over, the one named last changes fastest.
Arguments:
- features: bfloat16 [8, 24576, 512], P('dp', 'seq'), may hold values from -12 to 12, as said below
- slot_kind: int32 [8, 96], P('dp', 'seq'), may hold values from 0 to 2, as said below
- block_gain: float32 [512], replicated, may hold values from 0.1 to 1.9
- block_shift: float32 [512], replicated, may hold values from -2 to 2
- block_weight: bfloat16 [4608, 512], replicated, may hold values from -0.09375 to 0.09375
- block_bias: float32 [512], replicated, may hold values from -2 to 2
- final_gain: float32 [512], replicated, may hold values from 0.1 to 1.9
- final_shift: float32 [512], replicated, may hold values from -2 to 2
- latent_weight: bfloat16 [512, 144], replicated, may hold values from -0.09375 to 0.09375
- latent_bias: float32 [16], replicated, may hold values from -2 to 2
- embed_weight: bfloat16 [64, 1152], P(None, 'dp'), may hold values from -0.75 to 0.75
- embed_bias: bfloat16 [1152], P('dp'), may hold values from -2 to 2
Outputs:
- sequence: bfloat16 [8, 4096, 1152], P('dp', 'seq')
Inputs may be any that keep to these rules, and one draw needn't show every extreme that they name: `slot_kind`: the live slots of a device (kind 1 or 2) come before its empty ones. In every dp group, the live slots of the devices with seq index below d number between 2 d and 2 d + 2, and 2 * 32 over the whole group; in every group some device has 3 live slots. `features`: finite values.
All inputs are finite; a program needn't handle non-finite values.
Results may differ from a plain program's by a relative error of at most 0.014.
Values may be sent and summed in bfloat16 or wider, within the bound.
A program may use at most 64 MiB of HBM per device.

v0:
```python
import jax
import jax.numpy as jnp
from jax import lax
from jax.sharding import PartitionSpec as P

GROUPS = 32
SLOT_ROWS = 32
SLOT_COLS = 8
LATENT_SHIFT = 0.0609
LATENT_SCALE = 1.5305
NORM_EPSILON = 1e-06
OFFSETS = [(-1, -1), (-1, 0), (-1, 1), (0, -1), (0, 0), (0, 1), (1, -1), (1, 0), (1, 1)]


def shifted(value, axis, steps):
    count = lax.axis_size(axis)
    leading, last = (max(0, -steps), min(count, count - steps))
    return lax.ppermute(value, axis, [(source, source + steps) for source in range(leading, last)])


def group_norm(values, slot_types, norm_gain, norm_shift):
    slot_count, height, across, channels = values.shape
    grouped = values.reshape(slot_count, 2, height // 2, across, GROUPS, channels // GROUPS)
    joined = (slot_types == 2)[:, None, None, None, None, None]
    half_centre = jnp.mean(grouped, axis=(2, 3, 5), keepdims=True)
    centre = jnp.where(joined, jnp.mean(half_centre, axis=1, keepdims=True), half_centre)
    centred = grouped - centre
    half_spread = jnp.mean(centred * centred, axis=(2, 3, 5), keepdims=True)
    spread = jnp.where(joined, jnp.mean(half_spread, axis=1, keepdims=True), half_spread)
    normed = (centred * lax.rsqrt(spread + NORM_EPSILON)).reshape(values.shape)
    return normed * norm_gain + norm_shift


def boundary_mask(slot_types, height, row_step, out_type):
    row_index = jnp.arange(height)
    edge_row = height // 2 if row_step < 0 else height // 2 - 1
    crossing = (slot_types == 1)[:, None] & (row_index == edge_row)[None, :]
    return jnp.where(crossing, 0.0, 1.0).astype(out_type)[:, :, None, None]


def neighbour(padded, slot_types, row_step, col_step):
    height = padded.shape[1] - 2
    across = padded.shape[2] - 2
    window = padded[
        :, 1 + row_step : 1 + row_step + height, 1 + col_step : 1 + col_step + across, :
    ]
    if row_step != 0:
        window = window * boundary_mask(slot_types, height, row_step, window.dtype)
    return window


def encode(
    slots,
    slot_types,
    block_gain,
    block_shift,
    block_weight,
    block_bias,
    final_gain,
    final_shift,
    latent_weight,
    latent_bias,
):
    slot_count, height, across, channels = slots.shape
    lat_width = latent_weight.shape[1] // 9
    first_act = jax.nn.silu(
        group_norm(slots.astype(jnp.float32), slot_types, block_gain, block_shift)
    ).astype(jnp.bfloat16)
    padded = jnp.pad(first_act, ((0, 0), (1, 1), (1, 1), (0, 0)))
    columns = jnp.concatenate(
        [neighbour(padded, slot_types, row_step, col_step) for row_step, col_step in OFFSETS],
        axis=-1,
    )
    conv_out = (
        jnp.dot(columns.reshape(-1, 9 * channels), block_weight, preferred_element_type=jnp.float32)
        + block_bias
    )
    inner = (
        (slots.reshape(-1, channels).astype(jnp.float32) + conv_out)
        .astype(jnp.bfloat16)
        .reshape(slots.shape)
    )
    second_act = jax.nn.silu(
        group_norm(inner.astype(jnp.float32), slot_types, final_gain, final_shift)
    ).astype(jnp.bfloat16)
    tap_terms = jnp.dot(
        second_act.reshape(-1, channels), latent_weight, preferred_element_type=jnp.float32
    )
    tap_terms = tap_terms.reshape(slot_count, height, across, 9 * lat_width)
    padded_terms = jnp.pad(tap_terms, ((0, 0), (1, 1), (1, 1), (0, 0)))
    latent = jnp.zeros((slot_count, height, across, lat_width), jnp.float32) + latent_bias
    for tap_number, (row_step, col_step) in enumerate(OFFSETS):
        piece_terms = padded_terms[..., tap_number * lat_width : (tap_number + 1) * lat_width]
        latent = latent + neighbour(piece_terms, slot_types, row_step, col_step)
    scaled = (latent - LATENT_SHIFT) * LATENT_SCALE
    patches = scaled.reshape(slot_count, height // 2, 2, across // 2, 2, lat_width).transpose(
        0, 1, 3, 2, 4, 5
    )
    return patches.reshape(slot_count * (height // 2) * (across // 2), 4 * lat_width).astype(
        jnp.bfloat16
    )


def local(
    features,
    slot_kind,
    block_gain,
    block_shift,
    block_weight,
    block_bias,
    final_gain,
    final_shift,
    latent_weight,
    latent_bias,
    embed_weight,
    embed_bias,
):
    seq_devices = lax.axis_size("seq")
    position = lax.axis_index("seq")
    slot_total = slot_kind.shape[1]
    channels = features.shape[2]
    all_types = lax.all_gather(slot_kind[0], "seq", axis=0, tiled=True)
    live_slots = (all_types.reshape(seq_devices, slot_total) > 0).astype(jnp.int32)
    counts = jnp.sum(live_slots, axis=1)
    starts = jnp.cumsum(counts) - counts
    embed_full, bias_full = (
        lax.all_gather(embed_weight, "dp", axis=1, tiled=True),
        lax.all_gather(embed_bias, "dp", axis=0, tiled=True),
    )
    own_slots = features[0].reshape(slot_total, SLOT_ROWS, SLOT_COLS, channels)
    carry_in = starts[position] - 2 * position
    slot_number = jnp.arange(2, dtype=jnp.int32)
    hid_width = embed_full.shape[1]
    patches = encode(
        own_slots,
        slot_kind[0],
        block_gain,
        block_shift,
        block_weight,
        block_bias,
        final_gain,
        final_shift,
        latent_weight,
        latent_bias,
    )
    tokens = (
        (
            jnp.dot(patches, embed_full, preferred_element_type=jnp.float32)
            + bias_full.astype(jnp.float32)
        )
        .astype(jnp.bfloat16)
        .reshape(slot_total, -1, hid_width)
    )
    padded = jnp.concatenate([tokens, jnp.zeros_like(tokens[:1])], axis=0)
    arrived = shifted(lax.dynamic_slice_in_dim(padded, 2 - carry_in, 2, 0), "seq", 1)
    kept = jnp.take(tokens, jnp.maximum(slot_number - carry_in, 0), axis=0)
    incoming = (slot_number < carry_in).reshape((2,) + (1,) * (tokens.ndim - 1))
    result = jnp.where(incoming, arrived, kept)
    return result.reshape(1, -1, hid_width)


def solution(mesh):
    in_specs = (
        P("dp", "seq", None),
        P("dp", "seq"),
        P(),
        P(),
        P(),
        P(),
        P(),
        P(),
        P(),
        P(),
        P(None, "dp"),
        P("dp"),
    )
    out_specs = P("dp", "seq", None)
    return jax.shard_map(local, mesh=mesh, in_specs=in_specs, out_specs=out_specs, check_vma=False)
```

profile of v0, /device:TPU:32, one launch (start us, length us, event | category | flops | bytes accessed | tf_op | source)
XLA Modules:
  0.0 126.7 jit_solution(9587615518974002790)
XLA Ops:
  0.0 8.2 %reshape.311 = f32[3,2,16,8,32,16]{5,4,3,2,1,0:T(8,128)} reshape(bf16[1,768,512]{2,1,0:T(8,128)(2,1)} %param.12) | data formatting | bytes 2359296 | tf_op jit(solution)/shard_map/convert_element_type | solution.py:67
  8.2 0.2 convert_element_type.117
  8.4 0.4 copy-done.12
  8.9 5.9 %reduce_sum.82 = f32[3,2,32]{2,1,0:T(2,128)S(1)} reduce(f32[3,2,16,8,32,16]{5,4,3,2,1,0:T(8,128)} %reshape.311, f32[]{:T(128)} %constant.57.clone.1), dimensions={2,3,5}, to_apply=%region_2.3 | reduce | flops 393024 | bytes 1573636 | tf_op jit(solution)/shard_map/reduce_sum | solution.py:25
  14.8 0.1 broadcast_select_fusion.1
  14.8 6.4 %multiply_reduce_fusion.1 = f32[3,2,32]{2,1,0:T(2,128)S(1)} fusion(f32[3,2,16,8,32,16]{5,4,3,2,1,0:T(8,128)} %reshape.311, f32[3,2,32]{2,1,0:T(2,128)S(1)} %broadcast_select_fusion.1), kind=kLoop, calls=%fused_computation.2 | loop fusion | flops 1179456 | bytes 1574400 | tf_op jit(solution)/shard_map/reduce_sum | solution.py:28
  21.3 0.1 add_rsqrt_fusion.1
  21.4 0.3 mul.155
  21.6 1.1 mul.156
  22.7 0.2 sub.71
  23.0 1.7 %sub.72 = f32[3,32,512]{2,1,0:T(8,128)} reshape(f32[3,2,16,32,16]{4,3,2,1,0:T(8,128)S(1)} %sub.71) | data formatting | bytes 393216 | tf_op jit(solution)/shard_map/sub | solution.py:27
  24.7 0.1 and_select_fusion.1
  24.8 1.6 %multiply_convert_fusion.1 = bf16[3,32,8,512]{3,2,1,0:T(8,128)(2,1)S(1)} fusion(f32[3,32,8,512]{3,2,1,0:T(8,128)S(1)} %bitcast.64, f32[512]{0:T(512)S(1)} %copy-done.5, f32[512]{0:T(512)S(1)} %copy-done.6, f32[3,32,512]{2,1,0:T(8,128)S(1)} %mul.156, f32[3,32,512]{2,1,0:T(8,128)} %sub.72), kind=kLoop, calls=%fused_computation.28 | loop fusion | flops 3538944 | bytes 2756608 | tf_op jit(solution)/shard_map/convert_element_type | solution.py:68
  26.4 0.3 fusion.6
  26.6 0.2 fusion.8
  26.9 0.0 copy-start.3
  26.9 0.3 fusion.10
  27.2 0.2 fusion.11
  27.4 0.5 copy-done.3
  27.8 0.5 constant_dynamic-update-slice_fusion
  28.3 0.2 fusion.12
  28.5 0.3 fusion.14
  28.8 0.0 copy-start.2
  28.8 0.0 copy-start.10
  28.8 0.2 fusion.16
  29.1 0.3 fusion.18
  29.3 0.6 copy-done.2
  29.9 3.8 %fusion.4 = f32[768,512]{1,0:T(8,128)S(1)} fusion(bf16[768,4608]{1,0:T(8,128)(2,1)S(1)} %bitcast.71, bf16[4608,512]{1,0:T(8,128)(2,1)S(1)} %bitcast.75, f32[512]{0:T(512)S(1)} %copy-done.10, bf16[1,768,512]{2,1,0:T(8,128)(2,1)S(1)} %copy-done.2), kind=kOutput, calls=%fused_computation.29 | convolution fusion | flops 3625844736 | bytes 14157824 | tf_op jit(solution)/shard_map/dot_general | solution.py:75
  33.7 6.9 %reshape.312 = f32[3,2,16,8,32,16]{5,4,3,2,1,0:T(8,128)} reshape(f32[768,512]{1,0:T(8,128)S(1)} %fusion.4) | data formatting | bytes 3145728 | tf_op jit(solution)/shard_map/convert_element_type | solution.py:84
  40.6 5.9 %reduce_sum.86 = f32[3,2,32]{2,1,0:T(2,128)S(1)} reduce(f32[3,2,16,8,32,16]{5,4,3,2,1,0:T(8,128)} %reshape.312, f32[]{:T(128)} %constant.57.clone.1), dimensions={2,3,5}, to_apply=%region_6.7 | reduce | flops 393024 | bytes 1573636 | tf_op jit(solution)/shard_map/reduce_sum | solution.py:25
  46.5 0.1 broadcast_select_fusion
  46.6 6.4 %multiply_reduce_fusion = f32[3,2,32]{2,1,0:T(2,128)S(1)} fusion(f32[3,2,16,8,32,16]{5,4,3,2,1,0:T(8,128)} %reshape.312, f32[3,2,32]{2,1,0:T(2,128)S(1)} %broadcast_select_fusion), kind=kLoop, calls=%fused_computation.1 | loop fusion | flops 1179456 | bytes 1574400 | tf_op jit(solution)/shard_map/reduce_sum | solution.py:28
  53.0 0.1 add_rsqrt_fusion
  53.1 0.3 mul.171
  53.4 1.1 mul.172
  54.5 0.2 sub.77
  54.7 1.7 %sub.78 = f32[3,32,512]{2,1,0:T(8,128)} reshape(f32[3,2,16,32,16]{4,3,2,1,0:T(8,128)S(1)} %sub.77) | data formatting | bytes 393216 | tf_op jit(solution)/shard_map/sub | solution.py:27
  56.5 1.4 %multiply_convert_fusion = bf16[768,512]{1,0:T(8,128)(2,1)S(1)} fusion(f32[768,512]{1,0:T(8,128)S(1)} %fusion.4, f32[512]{0:T(512)S(1)} %copy-done.7, f32[512]{0:T(512)S(1)} %copy-done.8, f32[3,32,512]{2,1,0:T(8,128)S(1)} %mul.172, f32[3,32,512]{2,1,0:T(8,128)} %sub.78), kind=kLoop, calls=%fused_computation.27 | loop fusion | flops 3538944 | bytes 2756608 | tf_op jit(solution)/shard_map/convert_element_type | solution.py:85
  57.9 0.0 copy-start.14
  58.0 0.4 fusion.37
  58.3 0.0 copy-start.13
  58.4 1.0 fusion.36
  59.3 0.1 copy.22
  59.5 0.1 convert_element_type.113
  59.6 0.6 dynamic-slice.1
  60.9 0.2 dynamic-update-slice.1
  61.2 14.9 %all-reduce.4 = bf16[1152]{0:T(1024)(128)(2,1)S(1)} all-reduce(bf16[1152]{0:T(1024)(128)(2,1)S(1)} %dynamic-update-slice.1), channel_id=1, replica_groups=mesh['dp'=8,'seq'=32] {'dp'}, use_global_device_ids=true, to_apply=%add.4 | all-reduce | flops 1152 | bytes 4608
  76.0 12.8 %all-gather.1 = bf16[8,144,64]{1,2,0:T(8,128)(2,1)S(1)} all-gather(bf16[1,144,64]{1,2,0:T(8,128)(2,1)S(1)} %bitcast.72), channel_id=1, replica_groups=mesh['dp'=8,'seq'=32] {'dp'}, dimensions={0}, use_global_device_ids=true | all-gather | bytes 165888 | tf_op jit(solution)/shard_map/all_gather | solution.py:127
  88.9 0.1 copy.19
  89.0 0.3 reshape.337
  89.3 0.6 dynamic-slice
  90.5 0.1 bitcast_dynamic-update-slice_fusion
  90.6 22.4 %all-reduce.3 = s32[96]{0:T(128)S(1)} all-reduce(s32[96]{0:T(128)S(1)} %bitcast_dynamic-update-slice_fusion), channel_id=2, replica_groups=mesh['dp'=8,'seq'=32] {'seq'}, use_global_device_ids=true, to_apply=%add.3 | all-reduce | flops 96 | bytes 768
  113.1 0.1 reshape.308
  113.2 0.1 reduce_sum.81
  113.3 0.1 copy.17
  113.4 0.1 reduce-window.9
  113.5 0.1 reduce.4
  113.6 0.6 dynamic_slice.6
  114.8 0.3 fusion
  115.2 2.5 %collective-permute-start = (bf16[2,64,1152]{2,1,0:T(8,128)(2,1)S(1)}, bf16[2,64,1152]{2,1,0:T(8,128)(2,1)S(1)}, u32[]{:S(2)}, u32[]{:S(2)}) collective-permute-start(bf16[2,64,1152]{2,1,0:T(8,128)(2,1)S(1)} %pad_dynamic-slice_fusion), channel_id=1, source_target_pairs={{0,1},{1,2},{2,3},{3,4},{4,5},{5,6},{6,7},{7,8},{8,9},{9,10},{10,1... | collective-permute-start | bytes 884744 | tf_op jit(solution)/shard_map/ppermute | solution.py:18
  117.7 0.6 gather_fusion
  118.3 7.6 %collective-permute-done = bf16[2,64,1152]{2,1,0:T(8,128)(2,1)S(1)} collective-permute-done((bf16[2,64,1152]{2,1,0:T(8,128)(2,1)S(1)}, bf16[2,64,1152]{2,1,0:T(8,128)(2,1)S(1)}, u32[]{:S(2)}, u32[]{:S(2)}) %collective-permute-start) | collective-permute-done | bytes 294944 | tf_op jit(solution)/shard_map/ppermute | solution.py:18
  125.9 0.8 select_select_fusion
  (46 shorter events, 0.3 us)
Async XLA Ops:
  0.0 57.9 %copy-start = (bf16[512,144]{0,1:T(8,128)(2,1)S(1)}, bf16[512,144]{0,1:T(8,128)(2,1)}, u32[]{:S(2)}) copy-start(bf16[512,144]{0,1:T(8,128)(2,1)} %param.20) | copy-start | bytes 442372
  0.0 8.2 %copy-start.1 = (bf16[1,768,512]{2,1,0:T(8,128)(2,1)S(1)}, bf16[1,768,512]{2,1,0:T(8,128)(2,1)}, u32[]{:S(2)}) copy-start(bf16[1,768,512]{2,1,0:T(8,128)(2,1)} %param.12) | copy-start | bytes 2359300
  8.2 0.7 copy-start.12
  22.7 2.1 %copy-start.5 = (f32[512]{0:T(512)S(1)}, f32[512]{0:T(512)}, u32[]{:S(2)}) copy-start(f32[512]{0:T(512)} %param.15) | copy-start | bytes 6148
  22.7 2.1 %copy-start.6 = (f32[512]{0:T(512)S(1)}, f32[512]{0:T(512)}, u32[]{:S(2)}) copy-start(f32[512]{0:T(512)} %param.14) | copy-start | bytes 6148
  24.8 4.5 %slice-start = ((s8[4718592]{0:T(1024)(128)(4,1)}), s8[4194304]{0:T(1024)(128)(4,1)S(1)}, s32[]{:S(2)}) async-start(s8[4718592]{0:T(1024)(128)(4,1)} %bitcast.74), calls=%async_computation | async-start | bytes 8388608
  26.9 0.9 copy-start.3
  27.8 1.5 %slice-start.1 = ((s8[4718592]{0:T(1024)(128)(4,1)}), s8[524288]{0:T(1024)(128)(4,1)S(1)}, s32[]{:S(2)}) async-start(s8[4718592]{0:T(1024)(128)(4,1)} %bitcast.74), calls=%async_computation.1 | async-start | bytes 1048576
  28.8 1.1 copy-start.2
  28.8 1.1 copy-start.10
  54.4 2.0 %copy-start.7 = (f32[512]{0:T(512)S(1)}, f32[512]{0:T(512)}, u32[]{:S(2)}) copy-start(f32[512]{0:T(512)} %param.19) | copy-start | bytes 6148
  54.4 2.0 %copy-start.8 = (f32[512]{0:T(512)S(1)}, f32[512]{0:T(512)}, u32[]{:S(2)}) copy-start(f32[512]{0:T(512)} %param.18) | copy-start | bytes 6148
  56.5 1.9 %copy-start.9 = (f32[16]{0:T(128)S(1)}, f32[16]{0:T(128)}, u32[]{:S(2)}) copy-start(f32[16]{0:T(128)} %param.21) | copy-start | bytes 196
  57.9 1.7 %copy-start.14 = (u32[256]{0:T(256)S(1)}, u32[256]{0:T(256)}, u32[]{:S(2)}) copy-start(u32[256]{0:T(256)} %constant.85) | copy-start | bytes 3076
  57.9 3.0 %copy-start.11 = (bf16[144]{0:T(256)(128)(2,1)S(1)}, bf16[144]{0:T(256)(128)(2,1)}, u32[]{:S(2)}) copy-start(bf16[144]{0:T(256)(128)(2,1)} %param.23) | copy-start | bytes 868
  57.9 18.1 %copy-start.4 = (bf16[64,144]{1,0:T(8,128)(2,1)S(1)}, bf16[64,144]{1,0:T(8,128)(2,1)}, u32[]{:S(2)}) copy-start(bf16[64,144]{1,0:T(8,128)(2,1)} %param.22) | copy-start | bytes 55300
  58.3 30.9 %copy-start.13 = (u32[256]{0:T(256)S(1)}, u32[256]{0:T(256)}, u32[]{:S(2)}) copy-start(u32[256]{0:T(256)} %constant.80) | copy-start | bytes 3076
  115.2 10.7 %collective-permute-start = (bf16[2,64,1152]{2,1,0:T(8,128)(2,1)S(1)}, bf16[2,64,1152]{2,1,0:T(8,128)(2,1)S(1)}, u32[]{:S(2)}, u32[]{:S(2)}) collective-permute-start(bf16[2,64,1152]{2,1,0:T(8,128)(2,1)S(1)} %pad_dynamic-slice_fusion), channel_id=1, source_target_pairs={{0,1},{1,2},{2,3},{3,4},{4,5},{5,6},{6,7},{7,8},{8,9},{9,10},{10,1... | collective-permute-start | bytes 884744 | tf_op jit(solution)/shard_map/ppermute | solution.py:18
where the time goes:
time: 127 us
  blocking collectives  50.1 us (39%)
  other arithmetic  32.4 us (26%)
  local copies, waits for them, and re-layouts  27.3 us (21%)
  waiting for transfers between devices  7.57 us (6%)
  matrix products  4.42 us (3%)
  starting transfers between devices  2.51 us (2%)
  between operations  2.4 us (2%)
    unnamed x2, blocking collectives  37.3 us
    all_gather x1, blocking collectives, local(): lax.all_gather(embed_weight, 'dp', axis=1, tiled=True)  12.8 us
    reduce_sum x2, other arithmetic, group_norm(): half_spread = jnp.mean(centred * centred, axis=(2, 3, 5), keepdims=True)  12.8 us
    reduce_sum x2, other arithmetic, group_norm(): half_centre = jnp.mean(grouped, axis=(2, 3, 5), keepdims=True)  11.7 us
    convert_element_type x1, local copies, waits for them, and re-layouts, encode(): slots.astype(jnp.float32)  8.2 us
    ppermute x1, waiting for transfers between devices, shifted(): lax.ppermute(value, axis, [(source, source + steps) for source in range(l...  7.57 us
    convert_element_type x1, local copies, waits for them, and re-layouts, encode(): inner.astype(jnp.float32)  6.89 us
    sub x4, local copies, waits for them, and re-layouts, group_norm(): centred = grouped - centre  3.99 us
  transfers between devices with their start and end apart: 1, of which 1 were waited for; matrix products, arithmetic and copies ran while one was open for 0% of the time, Pallas kernels for 0%

commit v1 on v0

--- a/solution.py
+++ b/solution.py
@@ -10,6 +10,11 @@
 LATENT_SCALE = 1.5305
 NORM_EPSILON = 1e-06
 OFFSETS = [(-1, -1), (-1, 0), (-1, 1), (0, -1), (0, 0), (0, 1), (1, -1), (1, 0), (1, 1)]
+
+
+def swapped_in(x, mesh_axis, dim):
+    stack = jnp.stack([x] * lax.axis_size(mesh_axis))
+    return jnp.concatenate(lax.all_to_all(stack, mesh_axis, 0, 0), axis=dim)
 
 
 def shifted(value, axis, steps):
@@ -124,7 +129,7 @@
     counts = jnp.sum(live_slots, axis=1)
     starts = jnp.cumsum(counts) - counts
     embed_full, bias_full = (
-        lax.all_gather(embed_weight, "dp", axis=1, tiled=True),
+        swapped_in(embed_weight, "dp", 1),
         lax.all_gather(embed_bias, "dp", axis=0, tiled=True),
     )
     own_slots = features[0].reshape(slot_total, SLOT_ROWS, SLOT_COLS, channels)

time: 127 us -> 122 us (0.961)
  blocking collectives: 50.1 us -> 37.8 us
  starting transfers between devices: 2.51 us -> 6.98 us
  local copies, waits for them, and re-layouts: 27.3 us -> 30 us
    all_gather x1 -> x0, blocking collectives: 12.8 us -> none  [local(): lax.all_gather(embed_weight, 'dp', axis=1, tiled=True)]
    all_to_all x0 -> x1, starting transfers between devices: none -> 4.47 us  [swapped_in(): return jnp.concatenate(lax.all_to_all(stack, mesh_axis, 0, 0), axis=dim)]
    another operation x1 -> x2, local copies, waits for them, and re-layouts: 0.09 us -> 1.6 us  [the longest x1 1.51 us: swapped_in(): stack = jnp.stack([x] * lax.axis_size(mesh_axis))]
    reshape x0 -> x2, local copies, waits for them, and re-layouts: none -> 1.36 us  [swapped_in(): return jnp.concatenate(lax.all_to_all(stack, mesh_axis, 0, 0), axis=dim)]
    unnamed x43 -> x40, local copies, waits for them, and re-layouts: 3.69 us -> 3.59 us
  transfers between devices with their start and end apart: 1 -> 2, of which waited for: 1 -> 1; matrix products, arithmetic and copies ran while one was open for 0% -> 50% of each run, Pallas kernels for 0% -> 0%
where the time goes in v1:
time: 122 us
  blocking collectives  37.8 us (31%)
  other arithmetic  32.4 us (27%)
  local copies, waits for them, and re-layouts  30 us (25%)
  waiting for transfers between devices  7.57 us (6%)
  starting transfers between devices  6.98 us (6%)
  matrix products  4.43 us (4%)
  between operations  2.52 us (2%)
    unnamed x2, blocking collectives  37.8 us
    reduce_sum x2, other arithmetic, group_norm(): half_spread = jnp.mean(centred * centred, axis=(2, 3, 5), keepdims=True)  12.8 us
    reduce_sum x2, other arithmetic, group_norm(): half_centre = jnp.mean(grouped, axis=(2, 3, 5), keepdims=True)  11.7 us
    convert_element_type x1, local copies, waits for them, and re-layouts, encode(): slots.astype(jnp.float32)  8.2 us
    ppermute x1, waiting for transfers between devices, shifted(): lax.ppermute(value, axis, [(source, source + steps) for source in range(l...  7.57 us
    convert_element_type x1, local copies, waits for them, and re-layouts, encode(): inner.astype(jnp.float32)  6.89 us
    all_to_all x1, starting transfers between devices, swapped_in(): return jnp.concatenate(lax.all_to_all(stack, mesh_axis, 0, 0), axis=dim)  4.47 us
    sub x4, local copies, waits for them, and re-layouts, group_norm(): centred = grouped - centre  3.98 us
  transfers between devices with their start and end apart: 2, of which 1 were waited for; matrix products, arithmetic and copies ran while one was open for 50% of the time, Pallas kernels for 0%

profile of v1, /device:TPU:32, one launch (start us, length us, event | category | flops | bytes accessed | tf_op | source)
XLA Modules:
  0.0 121.6 jit_solution(14549827671538975500)
XLA Ops:
  0.0 1.5 %stack.2 = bf16[8,64,144]{2,1,0:T(8,128)(2,1)} broadcast(bf16[64,144]{1,0:T(8,128)(2,1)} %param.22), dimensions={1,2} | broadcast | bytes 165888 | tf_op jit(solution)/shard_map/stack | solution.py:16
  1.5 4.5 %all-to-all-start = ((bf16[8,64,144]{2,1,0:T(8,128)(2,1)}), bf16[8,64,144]{2,1,0:T(8,128)(2,1)}, u32[]{:S(2)}, u32[]{:S(2)}) async-start(bf16[8,64,144]{2,1,0:T(8,128)(2,1)} %stack.2), calls=%async_computation | async-start | bytes 524288 | tf_op jit(solution)/shard_map/all_to_all | solution.py:17
  6.0 8.2 %reshape.321 = f32[3,2,16,8,32,16]{5,4,3,2,1,0:T(8,128)} reshape(bf16[1,768,512]{2,1,0:T(8,128)(2,1)} %param.12) | data formatting | bytes 2359296 | tf_op jit(solution)/shard_map/convert_element_type | solution.py:72
  14.2 0.2 convert_element_type.117
  14.4 0.4 copy-done.11
  14.9 5.9 %reduce_sum.82 = f32[3,2,32]{2,1,0:T(2,128)S(1)} reduce(f32[3,2,16,8,32,16]{5,4,3,2,1,0:T(8,128)} %reshape.321, f32[]{:T(128)} %constant.57.clone.1), dimensions={2,3,5}, to_apply=%region_2.3 | reduce | flops 393024 | bytes 1573636 | tf_op jit(solution)/shard_map/reduce_sum | solution.py:30
  20.8 0.1 broadcast_select_fusion.1
  20.8 6.4 %multiply_reduce_fusion.1 = f32[3,2,32]{2,1,0:T(2,128)S(1)} fusion(f32[3,2,16,8,32,16]{5,4,3,2,1,0:T(8,128)} %reshape.321, f32[3,2,32]{2,1,0:T(2,128)S(1)} %broadcast_select_fusion.1), kind=kLoop, calls=%fused_computation.2 | loop fusion | flops 1179456 | bytes 1574400 | tf_op jit(solution)/shard_map/reduce_sum | solution.py:33
  27.3 0.1 add_rsqrt_fusion.1
  27.3 0.3 mul.155
  27.6 1.1 mul.156
  28.7 0.2 sub.71
  28.9 1.7 %sub.72 = f32[3,32,512]{2,1,0:T(8,128)} reshape(f32[3,2,16,32,16]{4,3,2,1,0:T(8,128)S(1)} %sub.71) | data formatting | bytes 393216 | tf_op jit(solution)/shard_map/sub | solution.py:32
  30.7 0.1 and_select_fusion.1
  30.8 1.6 %multiply_convert_fusion.1 = bf16[3,32,8,512]{3,2,1,0:T(8,128)(2,1)S(1)} fusion(f32[3,32,8,512]{3,2,1,0:T(8,128)S(1)} %bitcast.60, f32[512]{0:T(512)S(1)} %copy-done.4, f32[512]{0:T(512)S(1)} %copy-done.5, f32[3,32,512]{2,1,0:T(8,128)S(1)} %mul.156, f32[3,32,512]{2,1,0:T(8,128)} %sub.72), kind=kLoop, calls=%fused_computation.28 | loop fusion | flops 3538944 | bytes 2756608 | tf_op jit(solution)/shard_map/convert_element_type | solution.py:73
  32.4 0.3 fusion.6
  32.6 0.2 fusion.8
  32.9 0.3 fusion.10
  33.1 0.2 fusion.11
  33.3 0.5 copy-done.3
  33.8 0.5 constant_dynamic-update-slice_fusion
  34.3 0.2 fusion.12
  34.5 0.3 fusion.14
  34.8 0.0 copy-start.2
  34.8 0.0 copy-start.9
  34.8 0.2 fusion.16
  35.0 0.3 fusion.18
  35.3 0.6 copy-done.2
  35.9 3.8 %fusion.4 = f32[768,512]{1,0:T(8,128)S(1)} fusion(bf16[768,4608]{1,0:T(8,128)(2,1)S(1)} %bitcast.67, bf16[4608,512]{1,0:T(8,128)(2,1)S(1)} %bitcast.70, f32[512]{0:T(512)S(1)} %copy-done.9, bf16[1,768,512]{2,1,0:T(8,128)(2,1)S(1)} %copy-done.2), kind=kOutput, calls=%fused_computation.29 | convolution fusion | flops 3625844736 | bytes 14157824 | tf_op jit(solution)/shard_map/dot_general | solution.py:80
  39.7 6.9 %reshape.322 = f32[3,2,16,8,32,16]{5,4,3,2,1,0:T(8,128)} reshape(f32[768,512]{1,0:T(8,128)S(1)} %fusion.4) | data formatting | bytes 3145728 | tf_op jit(solution)/shard_map/convert_element_type | solution.py:89
  46.6 5.9 %reduce_sum.86 = f32[3,2,32]{2,1,0:T(2,128)S(1)} reduce(f32[3,2,16,8,32,16]{5,4,3,2,1,0:T(8,128)} %reshape.322, f32[]{:T(128)} %constant.57.clone.1), dimensions={2,3,5}, to_apply=%region_6.7 | reduce | flops 393024 | bytes 1573636 | tf_op jit(solution)/shard_map/reduce_sum | solution.py:30
  52.5 0.1 broadcast_select_fusion
  52.6 6.4 %multiply_reduce_fusion = f32[3,2,32]{2,1,0:T(2,128)S(1)} fusion(f32[3,2,16,8,32,16]{5,4,3,2,1,0:T(8,128)} %reshape.322, f32[3,2,32]{2,1,0:T(2,128)S(1)} %broadcast_select_fusion), kind=kLoop, calls=%fused_computation.1 | loop fusion | flops 1179456 | bytes 1574400 | tf_op jit(solution)/shard_map/reduce_sum | solution.py:33
  59.0 0.1 add_rsqrt_fusion
  59.1 0.3 mul.171
  59.4 1.1 mul.172
  60.4 0.2 sub.77
  60.7 1.7 %sub.78 = f32[3,32,512]{2,1,0:T(8,128)} reshape(f32[3,2,16,32,16]{4,3,2,1,0:T(8,128)S(1)} %sub.77) | data formatting | bytes 393216 | tf_op jit(solution)/shard_map/sub | solution.py:32
  62.4 1.4 %multiply_convert_fusion = bf16[768,512]{1,0:T(8,128)(2,1)S(1)} fusion(f32[768,512]{1,0:T(8,128)S(1)} %fusion.4, f32[512]{0:T(512)S(1)} %copy-done.6, f32[512]{0:T(512)S(1)} %copy-done.7, f32[3,32,512]{2,1,0:T(8,128)S(1)} %mul.172, f32[3,32,512]{2,1,0:T(8,128)} %sub.78), kind=kLoop, calls=%fused_computation.27 | loop fusion | flops 3538944 | bytes 2756608 | tf_op jit(solution)/shard_map/convert_element_type | solution.py:90
  63.9 0.0 copy-start.13
  63.9 0.0 copy-start.12
  63.9 0.4 fusion.37
  64.3 1.0 fusion.36
  65.3 0.1 copy.21
  65.4 0.1 convert_element_type.113
  65.6 0.7 dynamic-slice.1
  67.0 0.2 dynamic-update-slice.1
  67.2 15.4 %all-reduce.4 = bf16[1152]{0:T(1024)(128)(2,1)S(1)} all-reduce(bf16[1152]{0:T(1024)(128)(2,1)S(1)} %dynamic-update-slice.1), channel_id=1, replica_groups=mesh['dp'=8,'seq'=32] {'dp'}, use_global_device_ids=true, to_apply=%add.4 | all-reduce | flops 1152 | bytes 4608
  82.6 0.7 dynamic-slice
  84.0 0.1 bitcast_dynamic-update-slice_fusion
  84.1 22.4 %all-reduce.3 = s32[96]{0:T(128)S(1)} all-reduce(s32[96]{0:T(128)S(1)} %bitcast_dynamic-update-slice_fusion), channel_id=2, replica_groups=mesh['dp'=8,'seq'=32] {'seq'}, use_global_device_ids=true, to_apply=%add.3 | all-reduce | flops 96 | bytes 768
  106.5 0.1 reshape.318
  106.6 0.1 reduce_sum.81
  106.7 0.1 copy.16
  106.8 0.1 reduce-window.9
  106.9 0.1 reduce.4
  107.0 0.7 dynamic_slice.6
  108.4 1.1 copy.18
  109.5 0.3 reshape.315
  109.8 0.3 fusion
  110.1 2.5 %collective-permute-start = (bf16[2,64,1152]{2,1,0:T(8,128)(2,1)S(1)}, bf16[2,64,1152]{2,1,0:T(8,128)(2,1)S(1)}, u32[]{:S(2)}, u32[]{:S(2)}) collective-permute-start(bf16[2,64,1152]{2,1,0:T(8,128)(2,1)S(1)} %pad_dynamic-slice_fusion), channel_id=1, source_target_pairs={{0,1},{1,2},{2,3},{3,4},{4,5},{5,6},{6,7},{7,8},{8,9},{9,10},{10,1... | collective-permute-start | bytes 884744 | tf_op jit(solution)/shard_map/ppermute | solution.py:23
  112.6 0.6 gather_fusion
  113.2 7.6 %collective-permute-done = bf16[2,64,1152]{2,1,0:T(8,128)(2,1)S(1)} collective-permute-done((bf16[2,64,1152]{2,1,0:T(8,128)(2,1)S(1)}, bf16[2,64,1152]{2,1,0:T(8,128)(2,1)S(1)}, u32[]{:S(2)}, u32[]{:S(2)}) %collective-permute-start) | collective-permute-done | bytes 294944 | tf_op jit(solution)/shard_map/ppermute | solution.py:23
  120.8 0.8 select_select_fusion
  (46 shorter events, 0.3 us)
Async XLA Ops:
  0.0 63.9 %copy-start = (bf16[512,144]{0,1:T(8,128)(2,1)S(1)}, bf16[512,144]{0,1:T(8,128)(2,1)}, u32[]{:S(2)}) copy-start(bf16[512,144]{0,1:T(8,128)(2,1)} %param.20) | copy-start | bytes 442372
  1.5 106.9 %all-to-all-start = ((bf16[8,64,144]{2,1,0:T(8,128)(2,1)}), bf16[8,64,144]{2,1,0:T(8,128)(2,1)}, u32[]{:S(2)}, u32[]{:S(2)}) async-start(bf16[8,64,144]{2,1,0:T(8,128)(2,1)} %stack.2), calls=%async_computation | async-start | bytes 524288 | tf_op jit(solution)/shard_map/all_to_all | solution.py:17
  6.0 8.2 %copy-start.1 = (bf16[1,768,512]{2,1,0:T(8,128)(2,1)S(1)}, bf16[1,768,512]{2,1,0:T(8,128)(2,1)}, u32[]{:S(2)}) copy-start(bf16[1,768,512]{2,1,0:T(8,128)(2,1)} %param.12) | copy-start | bytes 2359300
  14.2 0.7 copy-start.11
  28.7 2.1 %copy-start.4 = (f32[512]{0:T(512)S(1)}, f32[512]{0:T(512)}, u32[]{:S(2)}) copy-start(f32[512]{0:T(512)} %param.15) | copy-start | bytes 6148
  28.7 2.1 %copy-start.5 = (f32[512]{0:T(512)S(1)}, f32[512]{0:T(512)}, u32[]{:S(2)}) copy-start(f32[512]{0:T(512)} %param.14) | copy-start | bytes 6148
  30.8 4.5 %slice-start = ((s8[4718592]{0:T(1024)(128)(4,1)}), s8[4194304]{0:T(1024)(128)(4,1)S(1)}, s32[]{:S(2)}) async-start(s8[4718592]{0:T(1024)(128)(4,1)} %bitcast.69), calls=%async_computation.1 | async-start | bytes 8388608
  32.9 0.9 copy-start.3
  33.8 1.5 %slice-start.1 = ((s8[4718592]{0:T(1024)(128)(4,1)}), s8[524288]{0:T(1024)(128)(4,1)S(1)}, s32[]{:S(2)}) async-start(s8[4718592]{0:T(1024)(128)(4,1)} %bitcast.69), calls=%async_computation.2 | async-start | bytes 1048576
  34.8 1.1 copy-start.2
  34.8 1.1 copy-start.9
  60.4 2.0 %copy-start.6 = (f32[512]{0:T(512)S(1)}, f32[512]{0:T(512)}, u32[]{:S(2)}) copy-start(f32[512]{0:T(512)} %param.19) | copy-start | bytes 6148
  60.4 2.0 %copy-start.7 = (f32[512]{0:T(512)S(1)}, f32[512]{0:T(512)}, u32[]{:S(2)}) copy-start(f32[512]{0:T(512)} %param.18) | copy-start | bytes 6148
  62.4 1.9 %copy-start.8 = (f32[16]{0:T(128)S(1)}, f32[16]{0:T(128)}, u32[]{:S(2)}) copy-start(f32[16]{0:T(128)} %param.21) | copy-start | bytes 196
  63.9 1.7 %copy-start.13 = (u32[256]{0:T(256)S(1)}, u32[256]{0:T(256)}, u32[]{:S(2)}) copy-start(u32[256]{0:T(256)} %constant.85) | copy-start | bytes 3076
  63.9 3.1 %copy-start.10 = (bf16[144]{0:T(256)(128)(2,1)S(1)}, bf16[144]{0:T(256)(128)(2,1)}, u32[]{:S(2)}) copy-start(bf16[144]{0:T(256)(128)(2,1)} %param.23) | copy-start | bytes 868
  63.9 18.7 %copy-start.12 = (u32[256]{0:T(256)S(1)}, u32[256]{0:T(256)}, u32[]{:S(2)}) copy-start(u32[256]{0:T(256)} %constant.80) | copy-start | bytes 3076
  110.1 10.7 %collective-permute-start = (bf16[2,64,1152]{2,1,0:T(8,128)(2,1)S(1)}, bf16[2,64,1152]{2,1,0:T(8,128)(2,1)S(1)}, u32[]{:S(2)}, u32[]{:S(2)}) collective-permute-start(bf16[2,64,1152]{2,1,0:T(8,128)(2,1)S(1)} %pad_dynamic-slice_fusion), channel_id=1, source_target_pairs={{0,1},{1,2},{2,3},{3,4},{4,5},{5,6},{6,7},{7,8},{8,9},{9,10},{10,1... | collective-permute-start | bytes 884744 | tf_op jit(solution)/shard_map/ppermute | solution.py:23
